TPU v7x, 32 devices: a whole 2x2x4 slice. The times are simulated.
32 devices in a mesh: heads: 8 (over y, x, core), batch: 4 (over z).
Axes of the slice: x: 2, y: 2, z: 4, core: 2. Of those that a mesh axis runs over, the one named last changes fastest.
Arguments:
- tokens: bfloat16 [2, 4, 1024, 2048], P(None, 'batch', 'heads'), may hold values from -6 to 6
- cotangent: bfloat16 [2, 4, 1024, 2048], P(None, 'batch', 'heads'), may hold values from -6 to 6
- doc_lengths: int32 [2, 4, 4], P(None, 'batch'), may hold values from 1 to 768, 1024 in all within a row
- pad_mask: int32 [2, 4, 1024], P(None, 'batch'), may hold values 0 or 1
- w_query: bfloat16 [2048, 1024], P(None, 'heads'), may hold values from -0.1875 to 0.1875
- w_key: bfloat16 [2048, 1024], P(None, 'heads'), may hold values from -0.1875 to 0.1875
- w_value: bfloat16 [2048, 1024], P(None, 'heads'), may hold values from -0.125 to 0.125
- w_out: bfloat16 [1024, 2048], P('heads'), may hold values from -0.75 to 0.75
- w_gate: bfloat16 [2048, 8192], P(None, 'heads'), may hold values from -0.125 to 0.125
- w_up: bfloat16 [2048, 8192], P(None, 'heads'), may hold values from -0.125 to 0.125
- w_down: bfloat16 [8192, 2048], P('heads'), may hold values from -0.0625 to 0.0625
- norm_attn: float32 [2048], replicated, may hold values from 0.1 to 1.9
- norm_mlp: float32 [2048], replicated, may hold values from 0.1 to 1.9
- mix_gate: float32 [8], P('heads'), may hold values from -2 to 2
Outputs:
- layer_out: bfloat16 [2, 4, 1024, 2048], P(None, 'batch', 'heads')
- grad_tokens: float32 [2, 4, 1024, 2048], P(None, 'batch', 'heads')
- grad_w_query: float32 [2048, 1024], P(None, 'heads')
- grad_w_key: float32 [2048, 1024], P(None, 'heads')
- grad_w_value: float32 [2048, 1024], P(None, 'heads')
- grad_w_out: float32 [1024, 2048], P('heads')
- grad_w_gate: float32 [2048, 8192], P(None, 'heads')
- grad_w_up: float32 [2048, 8192], P(None, 'heads')
- grad_w_down: float32 [8192, 2048], P('heads')
- grad_norm_attn: float32 [2048], replicated
- grad_norm_mlp: float32 [2048], replicated
- grad_mix_gate: float32 [8], P('heads')
Inputs may be any that keep to these rules, and one draw needn't show every extreme that they name: `doc_lengths`: the 4 lengths of a sequence sum to 1024; the longest is 768.
All inputs are finite; a program needn't handle non-finite values. No bound on the sum of `pad_mask` on one device may be relied on, other than what follows from the above.
Results may differ from a plain program's by a relative error of at most 0.018.
Values may be sent and summed in bfloat16 or wider, within the bound.
No kernel may reach another device: no remote copies, remote signals or barrier semaphores. Data moves between devices by JAX's collectives and lax.ppermute only.
A program may use at most 256 MiB of HBM per device.

v0:
```python
import jax
import jax.numpy as jnp
from jax import lax
from jax.sharding import PartitionSpec as P

DH = 128
SEG = 512
SEGS = 2
LEN = 1024
MICRO = 2
epsilon = 1e-05
big_negative = -1e30


def dot_rows(left_mat, right_mat):
    return lax.dot_general(
        left_mat, right_mat, (((1,), (1,)), ((), ())), preferred_element_type=jnp.float32
    )


def dot_cols(left_mat, right_mat):
    return lax.dot_general(
        left_mat, right_mat, (((0,), (0,)), ((), ())), preferred_element_type=jnp.float32
    )


def batch_mm(left, right):
    return lax.dot_general(
        left, right, (((2,), (1,)), ((0,), (0,))), preferred_element_type=jnp.float32
    )


def batch_mt(left, right):
    return lax.dot_general(
        left, right, (((2,), (2,)), ((0,), (0,))), preferred_element_type=jnp.float32
    )


def batch_tm(left, right):
    return lax.dot_general(
        left, right, (((1,), (1,)), ((0,), (0,))), preferred_element_type=jnp.float32
    )


def norm_scale(row_block):
    return lax.rsqrt(jnp.mean(row_block * row_block, axis=-1, keepdims=True) + epsilon)


def norm_back(row_block, row_scale, gain_vec, upstream):
    shaped = upstream * gain_vec
    inner = jnp.mean(shaped * row_block, axis=-1, keepdims=True)
    d_rows = row_scale * shaped - row_block * row_scale * row_scale * row_scale * inner
    d_gain = jnp.sum(upstream * row_block * row_scale, axis=0)
    return (d_rows, d_gain)


def positive(values_in):
    return jnp.where(values_in > 0, values_in + 1.0, jnp.exp(values_in))


def local_mask(begin_row, positions, doc_ids, valid_keys):
    seg_pos = positions[begin_row : begin_row + SEG]
    seg_doc = doc_ids[:, begin_row : begin_row + SEG]
    seg_valid = valid_keys[:, begin_row : begin_row + SEG]
    same_doc = seg_doc[:, :, None] == seg_doc[:, None, :]
    causal = (seg_pos[None, :] <= seg_pos[:, None])[None]
    diagonal = (seg_pos[None, :] == seg_pos[:, None])[None]
    return same_doc & causal & (seg_valid[:, None, :] | diagonal)


def memory_mask(begin_row, doc_ids, valid_keys):
    seg_doc = doc_ids[:, begin_row : begin_row + SEG]
    return (seg_doc[:, :, None] == doc_ids[:, None, :begin_row]) & valid_keys[:, None, :begin_row]


def head_forward(query_all, key_all, value_all, share, positions, doc_ids, valid_keys):
    score_scale = DH ** (-0.5)
    pos_query = positive(query_all.astype(jnp.float32)).astype(jnp.bfloat16)
    pos_key = positive(key_all.astype(jnp.float32)).astype(jnp.bfloat16)
    kept = []
    dotted_parts, recalled_parts = ([], [])
    for segment in range(SEGS):
        rows = slice(segment * SEG, (segment + 1) * SEG)
        before = slice(0, segment * SEG)
        allowed = local_mask(segment * SEG, positions, doc_ids, valid_keys)
        scores = jnp.where(
            allowed, batch_mt(query_all[:, rows], key_all[:, rows]) * score_scale, big_negative
        )
        shifted = jnp.exp(scores - jnp.max(scores, axis=2, keepdims=True))
        soft_probs = shifted / jnp.sum(shifted, axis=2, keepdims=True)
        dotted_parts.append(batch_mm(soft_probs.astype(jnp.bfloat16), value_all[:, rows]))
        if segment == 0:
            recalled_parts.append(jnp.zeros((query_all.shape[0], SEG, DH), jnp.float32))
            kept.append((soft_probs,))
        else:
            mem_allowed = memory_mask(segment * SEG, doc_ids, valid_keys)
            weights = jnp.where(mem_allowed, batch_mt(pos_query[:, rows], pos_key[:, before]), 0.0)
            row_total = jnp.sum(weights, axis=2, keepdims=True)
            denominator = jnp.maximum(row_total, 1.0)
            weights_low = weights.astype(jnp.bfloat16)
            numerator = batch_mm(weights_low, value_all[:, before])
            recalled_parts.append(numerator / denominator)
            kept.append((soft_probs, mem_allowed, row_total, weights_low, numerator))
    dotted = jnp.concatenate(dotted_parts, axis=1)
    recalled = jnp.concatenate(recalled_parts, axis=1)
    mixed_head = share * recalled + (1.0 - share) * dotted
    return (mixed_head, dotted, recalled, pos_query, pos_key, kept)


def head_backward(query_all, key_all, value_all, share, d_mixed, forward_kept):
    _, dotted, recalled, pos_query, pos_key, kept = forward_kept
    score_scale = DH ** (-0.5)
    query_float = query_all.astype(jnp.float32)
    key_float = key_all.astype(jnp.float32)
    d_share = jnp.sum(d_mixed * (recalled - dotted)) * share * (1.0 - share)
    d_dotted = ((1.0 - share) * d_mixed).astype(jnp.bfloat16)
    d_recalled = share * d_mixed
    nothing = jnp.zeros((query_all.shape[0], SEG, DH), jnp.float32)
    d_query, d_key, d_value, d_posq, d_posk = [[nothing for _ in range(SEGS)] for _ in range(5)]
    for segment in range(SEGS):
        rows = slice(segment * SEG, (segment + 1) * SEG)
        before = slice(0, segment * SEG)
        soft_probs = kept[segment][0]
        d_dot_seg = d_dotted[:, rows]
        d_value[segment] += batch_tm(soft_probs.astype(jnp.bfloat16), d_dot_seg)
        d_probs = batch_mt(d_dot_seg, value_all[:, rows])
        d_scores = (
            soft_probs * (d_probs - jnp.sum(soft_probs * d_probs, axis=2, keepdims=True))
        ).astype(jnp.bfloat16)
        d_query[segment] += batch_mm(d_scores, key_all[:, rows]) * score_scale
        d_key[segment] += batch_tm(d_scores, query_all[:, rows]) * score_scale
        if segment > 0:
            _, mem_allowed, row_total, weights_low, numerator = kept[segment]
            denominator = jnp.maximum(row_total, 1.0)
            d_recall_seg = d_recalled[:, rows]
            d_numer = (d_recall_seg / denominator).astype(jnp.bfloat16)
            d_denom = jnp.where(
                row_total > 1.0,
                -jnp.sum(d_recall_seg * numerator, axis=2, keepdims=True)
                / (denominator * denominator),
                0.0,
            )
            d_weights = jnp.where(
                mem_allowed, batch_mt(d_numer, value_all[:, before]) + d_denom, 0.0
            ).astype(jnp.bfloat16)
            d_posq[segment] += batch_mm(d_weights, pos_key[:, before])
            d_posk_all = batch_tm(d_weights, pos_query[:, rows])
            d_value_all = batch_tm(weights_low, d_numer)
            for earlier in range(segment):
                part = slice(earlier * SEG, (earlier + 1) * SEG)
                d_posk[earlier] += d_posk_all[:, part]
                d_value[earlier] += d_value_all[:, part]
    d_query, d_key, d_value, d_posq, d_posk = [
        jnp.concatenate(parts, axis=1) for parts in (d_query, d_key, d_value, d_posq, d_posk)
    ]
    d_query = d_query + d_posq * jnp.where(query_float > 0, 1.0, jnp.exp(query_float))
    d_key = d_key + d_posk * jnp.where(key_float > 0, 1.0, jnp.exp(key_float))
    return (
        d_query.astype(jnp.bfloat16),
        d_key.astype(jnp.bfloat16),
        d_value.astype(jnp.bfloat16),
        d_share,
    )


class Chain:

    def __init__(self, axis, size, depth):
        self.axis, self.size, self.depth = (axis, size, depth)
        self.place = lax.axis_index(axis)
        half = size // 2
        self.stages = [("in", [(s - 1, s), (size - s, size - 1 - s)]) for s in range(1, half)]
        self.stages.append(("in", [(half - 1, half), (half, half - 1)]))
        self.stages += [
            ("out", [(s, s - 1), (size - 1 - s, size - s)]) for s in range(half - 1, 0, -1)
        ]
        self.entered = []
        self.last = [None] * len(self.stages)

    def add(self, array):
        if self.size == 1:
            return array
        if self.size % 2:
            return lax.psum(array, self.axis)
        if len(self.entered) >= self.depth:
            array, _ = lax.optimization_barrier((array, self.entered[-self.depth]))
        for number, (kind, pairs) in enumerate(self.stages):
            arrived = lax.ppermute(array, self.axis, pairs)
            if self.last[number] is not None:
                array, arrived, _ = lax.optimization_barrier((array, arrived, self.last[number]))
            if kind == "in":
                array = array + arrived
            else:
                receives = jnp.zeros((), jnp.bool_)
                for _, target in pairs:
                    receives = receives | (self.place == target)
                array = jnp.where(receives, arrived, array)
            self.last[number] = array
            if number == 0:
                self.entered.append(array)
        return array


def per_device(
    tokens,
    cotangent,
    doc_lengths,
    pad_mask,
    w_query,
    w_key,
    w_value,
    w_out,
    w_gate,
    w_up,
    w_down,
    norm_attn,
    norm_mlp,
    mix_gate,
    *,
    n_heads,
    n_batch
):
    width = tokens.shape[-1]
    rows = tokens.shape[2]
    own_rows = MICRO * rows
    all_rows = n_heads * own_rows
    hidden_cols = w_gate.shape[1]
    here = lax.axis_index("heads")
    low = jnp.bfloat16

    def by_sequence(array):
        cols = array.shape[-1]
        return (
            array.reshape(n_heads, MICRO, rows, cols)
            .transpose(1, 0, 2, 3)
            .reshape(MICRO, LEN, cols)
        )

    def by_device(array):
        cols = array.shape[-1]
        return (
            array.reshape(MICRO, n_heads, rows, cols).transpose(1, 0, 2, 3).reshape(all_rows, cols)
        )

    def gather(array):
        return lax.all_gather(array, "heads", axis=0, tiled=True)

    def scatter(array):
        return lax.psum_scatter(array, "heads", scatter_dimension=0, tiled=True)

    def own(array):
        return lax.dynamic_slice_in_dim(array, here * own_rows, own_rows, 0)

    w_qkv = jnp.concatenate([w_query, w_key, w_value], axis=1)
    w_gate_up = jnp.concatenate([w_gate, w_up], axis=1)
    share = jax.nn.sigmoid(mix_gate)[0]
    positions = jnp.arange(LEN, dtype=jnp.int32)
    doc_ends = jnp.cumsum(doc_lengths[:, 0], axis=1)
    doc_ids = jnp.sum((positions[None, :, None] >= doc_ends[:, None, :]).astype(jnp.int32), axis=2)
    valid_keys = pad_mask[:, 0] == 1
    tok_own = tokens.reshape(own_rows, width)
    cot_own = cotangent.reshape(own_rows, width)
    tok_all = gather(tok_own)
    w_out_all = gather(w_out)
    x_all = tok_all.astype(jnp.float32)
    h1_all = (x_all * norm_scale(x_all) * norm_attn).astype(low)
    qkv = jnp.dot(h1_all, w_qkv, preferred_element_type=jnp.float32).astype(low)
    query, key, value = [by_sequence(qkv[:, i * DH : (i + 1) * DH]) for i in range(3)]
    head_kept = head_forward(query, key, value, share, positions, doc_ids, valid_keys)
    mixed = by_device(head_kept[0].astype(low))
    mixed_all = lax.all_gather(mixed, "heads", axis=1, tiled=True)
    cot_all = gather(cot_own)
    y1_all = x_all + jnp.dot(mixed_all, w_out_all, preferred_element_type=jnp.float32)
    h2_all = (y1_all * norm_scale(y1_all) * norm_mlp).astype(low)
    x_own = tok_own.astype(jnp.float32)
    y1_own = own(y1_all)
    gate_up = jnp.dot(h2_all, w_gate_up, preferred_element_type=jnp.float32)
    gate_pre = gate_up[:, :hidden_cols]
    up_pre = gate_up[:, hidden_cols:]
    sig_gate = jax.nn.sigmoid(gate_pre)
    hidden = (gate_pre * sig_gate * up_pre).astype(low)
    d_hidden = dot_rows(cot_all, w_down)
    d_up = d_hidden * gate_pre * sig_gate
    d_gate = d_hidden * up_pre * sig_gate * (1.0 + gate_pre * (1.0 - sig_gate))
    d_gate_up = jnp.concatenate([d_gate, d_up], axis=1).astype(low)
    chain = Chain("batch", n_batch, 3)
    d_h2 = scatter(dot_rows(d_gate_up, w_gate_up).astype(low)).astype(jnp.float32)
    down_parts, gate_up_parts = ([], [])
    step = hidden_cols // 4
    for begin in range(0, hidden_cols, step):
        down_parts.append(chain.add(dot_cols(hidden[:, begin : begin + step], cot_all).astype(low)))
    step = width // 8
    for begin in range(0, width, step):
        gate_up_parts.append(
            chain.add(dot_cols(h2_all[:, begin : begin + step], d_gate_up).astype(low))
        )
    mlp_own = scatter(jnp.dot(hidden, w_down, preferred_element_type=jnp.float32).astype(low))
    layer_out = (y1_own + mlp_own.astype(jnp.float32)).astype(low)
    scale_mlp = norm_scale(y1_own)
    d_y1, gain_mlp_part = norm_back(y1_own, scale_mlp, norm_mlp, d_h2)
    d_y1 = d_y1 + cot_own.astype(jnp.float32)
    d_attn = d_y1.astype(low)
    d_mixed_own = dot_rows(d_attn, w_out_all).astype(low)
    d_mixed = lax.all_to_all(d_mixed_own, "heads", split_axis=1, concat_axis=0, tiled=True)
    grad_out = scatter(dot_cols(own(mixed_all), d_attn).astype(low))
    d_query, d_key, d_value, d_share = head_backward(
        query, key, value, share, by_sequence(d_mixed).astype(jnp.float32), head_kept
    )
    d_qkv = jnp.concatenate([by_device(d_query), by_device(d_key), by_device(d_value)], axis=1)
    d_h1 = scatter(dot_rows(d_qkv, w_qkv).astype(low)).astype(jnp.float32)
    grad_out = chain.add(grad_out)
    grad_qkv = chain.add(dot_cols(h1_all, d_qkv).astype(low))
    d_x, gain_attn_part = norm_back(x_own, norm_scale(x_own), norm_attn, d_h1)
    grad_tokens = (d_x + d_y1).reshape(tokens.shape)
    slots = jnp.where(jnp.arange(n_heads) == here, d_share, 0.0)
    sums = lax.psum(jnp.concatenate([gain_attn_part, gain_mlp_part, slots]), ("heads", "batch"))
    grad_mix = lax.dynamic_slice_in_dim(sums, 2 * width + here, 1, 0)
    wide = jnp.float32
    grad_qkv = grad_qkv.astype(wide)
    grad_gate_up = jnp.concatenate([p.astype(wide) for p in gate_up_parts], axis=0)
    grad_down = jnp.concatenate([p.astype(wide) for p in down_parts], axis=0)
    return (
        layer_out.reshape(tokens.shape),
        grad_tokens,
        grad_qkv[:, :DH],
        grad_qkv[:, DH : 2 * DH],
        grad_qkv[:, 2 * DH :],
        grad_out.astype(wide),
        grad_gate_up[:, :hidden_cols],
        grad_gate_up[:, hidden_cols:],
        grad_down,
        sums[:width],
        sums[width : 2 * width],
        grad_mix,
    )


def solution(mesh):
    in_specs = (
        P(None, "batch", "heads", None),
        P(None, "batch", "heads", None),
        P(None, "batch", None),
        P(None, "batch", None),
        P(None, "heads"),
        P(None, "heads"),
        P(None, "heads"),
        P("heads", None),
        P(None, "heads"),
        P(None, "heads"),
        P("heads", None),
        P(),
        P(),
        P("heads"),
    )
    out_specs = (
        P(None, "batch", "heads", None),
        P(None, "batch", "heads", None),
        P(None, "heads"),
        P(None, "heads"),
        P(None, "heads"),
        P("heads", None),
        P(None, "heads"),
        P(None, "heads"),
        P("heads", None),
        P(),
        P(),
        P("heads"),
    )

    def program(*arrays):
        return per_device(*arrays, n_heads=mesh.shape["heads"], n_batch=mesh.shape["batch"])

    return jax.shard_map(
        program, mesh=mesh, in_specs=in_specs, out_specs=out_specs, check_vma=False
    )
```

profile of v0, /device:TPU:0, one launch (start us, length us, event | category | flops | bytes accessed | tf_op | source)
XLA Modules:
  0.0 852.9 jit_solution(9633711189530872917)
XLA Ops:
  16.1 50.9 %all-gather.5.cloned.1.call-done = bf16[2048,2048]{1,0:T(8,128)(2,1)} async-done(((bf16[256,2048]{1,0:T(8,128)(2,1)}), bf16[2048,2048]{1,0:T(8,128)(2,1)}) %all-gather.5.cloned.1.call-update) | async-done | bytes 8388624 | tf_op jit(solution)/shard_map/all_gather | solution.py:246
  105.7 39.9 %all-gather.7.cloned.1.call-done = bf16[2048,1024]{1,0:T(8,128)(2,1)} async-done(((bf16[2048,128]{1,0:T(8,128)(2,1)}), bf16[2048,1024]{1,0:T(8,128)(2,1)}) %all-gather.7.cloned.1.call-update) | async-done | bytes 4194320 | tf_op jit(solution)/shard_map/all_gather | solution.py:271
  145.6 13.5 %multiply_reduce_fusion = (f32[2048]{0:T(1024)S(1)}, f32[2048,2048]{1,0:T(8,128)S(1)}) fusion(bf16[2048,1024]{1,0:T(8,128)(2,1)} %all-gather.7.cloned.1.call-done, bf16[1024,2048]{1,0:T(8,128)(2,1)} %all-gather.9.cloned.1.call-done, bf16[2048,2048]{1,0:T(8,128)(2,1)} %all-gather.5.cloned.1.call-done), kind=kOutput, calls=%fused_computation.9 | convolution fusion | flops 8606709760 | bytes 33562624 | tf_op jit(solution)/shard_map/dot_general | solution.py:273
  169.3 24.3 %fusion.125 = f32[2048,2048]{0,1:T(8,128)} fusion(bf16[2048,2048]{1,0:T(8,128)(2,1)} %multiply_convert_fusion, bf16[2048,2048]{1,0:T(8,128)(2,1)} %constant_dynamic-update-slice_fusion.3), kind=kOutput, calls=%fused_computation.223 | convolution fusion | flops 17179869184 | bytes 33554432 | tf_op jit(solution)/shard_map/dot_general | solution.py:277
  193.7 8.1 all-gather.11.cloned.1.call-done
  201.8 22.8 %multiply_convert_fusion.2 = (bf16[2048,1024]{0,1:T(8,128)(2,1)S(1)}, bf16[2048,1024]{0,1:T(8,128)(2,1)}, bf16[2048,1024]{0,1:T(8,128)(2,1)}) fusion(f32[2048,2048]{0,1:T(8,128)} %fusion.125, bf16[2048,2048]{1,0:T(8,128)(2,1)} %all-gather.11.cloned.1.call-done, bf16[1024,2048]{1,0:T(8,128)(2,1)} %param.24), kind=kOutput, calls=%fused_computation.12 | convolution fusion | flops 8623489024 | bytes 41943040 | tf_op jit(solution)/shard_map/dot_general | solution.py:16
  226.6 22.9 %convolution_convert_fusion.1 = bf16[2048,2048]{1,0:T(8,128)(2,1)} fusion(bf16[2048,2048]{1,0:T(8,128)(2,1)} %constant_dynamic-update-slice_fusion.3, bf16[2048,1024]{0,1:T(8,128)(2,1)} %get-tuple-element.249, bf16[2048,1024]{0,1:T(8,128)(2,1)S(1)} %get-tuple-element.248), kind=kOutput, calls=%fused_computation.16 | convolution fusion | flops 17200840704 | bytes 25165824 | tf_op jit(solution)/shard_map/dot_general | solution.py:16
  249.6 14.5 %convolution_convert_fusion.2 = bf16[2048,2048]{1,0:T(8,128)(2,1)} fusion(bf16[2048,1024]{0,1:T(8,128)(2,1)} %get-tuple-element.252, bf16[1024,2048]{1,0:T(8,128)(2,1)} %param.24), kind=kOutput, calls=%fused_computation.17 | convolution fusion | flops 8594128896 | bytes 16777216 | tf_op jit(solution)/shard_map/dot_general | solution.py:297
  276.5 6.4 convolution_convert_fusion.14
  298.1 7.1 convolution_convert_fusion.16
  310.1 7.2 convolution_convert_fusion.7
  339.8 56.7 %reduce-scatter.5.cloned.1.call-done = bf16[256,2048]{1,0:T(8,128)(2,1)} async-done(((bf16[2048,2048]{1,0:T(8,128)(2,1)}), bf16[256,2048]{1,0:T(8,128)(2,1)}) %reduce-scatter.5.cloned.1.call-update) | async-done | bytes 1048592 | tf_op jit(solution)/shard_map/reduce_scatter | solution.py:249
  407.6 7.1 convolution_convert_fusion.8
  460.1 6.8 convolution_convert_fusion
  468.1 6.6 convolution_convert_fusion.17
  481.1 11.4 %collective-permute-start.6 = (bf16[256,2048]{1,0:T(8,128)(2,1)S(1)}, bf16[256,2048]{1,0:T(8,128)(2,1)S(1)}, u32[]{:S(2)}, u32[]{:S(2)}) collective-permute-start(bf16[256,2048]{1,0:T(8,128)(2,1)S(1)} %copy-done.22), channel_id=1, source_target_pairs={{0,1},{3,2},{4,5},{7,6},{8,9},{11,10},{12,13},{15,14},{16,17},{19,... | collective-permute-start | bytes 3145736 | tf_op jit(solution)/shard_map/ppermute | solution.py:188
  507.4 8.6 %collective-permute-done.6 = bf16[256,2048]{1,0:T(8,128)(2,1)S(1)} collective-permute-done((bf16[256,2048]{1,0:T(8,128)(2,1)S(1)}, bf16[256,2048]{1,0:T(8,128)(2,1)S(1)}, u32[]{:S(2)}, u32[]{:S(2)}) %collective-permute-start.6) | collective-permute-done | bytes 1048608 | tf_op jit(solution)/shard_map/ppermute | solution.py:188
  519.4 19.1 %collective-permute-done.5 = bf16[256,2048]{1,0:T(8,128)(2,1)S(1)} collective-permute-done((bf16[256,2048]{1,0:T(8,128)(2,1)S(1)}, bf16[256,2048]{1,0:T(8,128)(2,1)S(1)}, u32[]{:S(2)}, u32[]{:S(2)}) %collective-permute-start.5) | collective-permute-done | bytes 1048608 | tf_op jit(solution)/shard_map/ppermute | solution.py:188
  540.9 18.1 %collective-permute-done.10 = bf16[256,2048]{1,0:T(8,128)(2,1)S(1)} collective-permute-done((bf16[256,2048]{1,0:T(8,128)(2,1)S(1)}, bf16[256,2048]{1,0:T(8,128)(2,1)S(1)}, u32[]{:S(2)}, u32[]{:S(2)}) %collective-permute-start.10) | collective-permute-done | bytes 1048608 | tf_op jit(solution)/shard_map/ppermute | solution.py:188
  561.0 8.7 %collective-permute-done.37 = bf16[256,2048]{1,0:T(8,128)(2,1)S(1)} collective-permute-done((bf16[256,2048]{1,0:T(8,128)(2,1)S(1)}, bf16[256,2048]{1,0:T(8,128)(2,1)S(1)}, u32[]{:S(2)}, u32[]{:S(2)}) %collective-permute-start.37) | collective-permute-done | bytes 1048608 | tf_op jit(solution)/shard_map/ppermute | solution.py:188
  571.2 19.0 %collective-permute-done.36 = bf16[256,2048]{1,0:T(8,128)(2,1)S(1)} collective-permute-done((bf16[256,2048]{1,0:T(8,128)(2,1)S(1)}, bf16[256,2048]{1,0:T(8,128)(2,1)S(1)}, u32[]{:S(2)}, u32[]{:S(2)}) %collective-permute-start.36) | collective-permute-done | bytes 1048608 | tf_op jit(solution)/shard_map/ppermute | solution.py:188
  600.2 14.9 %collective-permute-done.8 = bf16[256,2048]{1,0:T(8,128)(2,1)S(1)} collective-permute-done((bf16[256,2048]{1,0:T(8,128)(2,1)S(1)}, bf16[256,2048]{1,0:T(8,128)(2,1)S(1)}, u32[]{:S(2)}, u32[]{:S(2)}) %collective-permute-start.8) | collective-permute-done | bytes 1048608 | tf_op jit(solution)/shard_map/ppermute | solution.py:188
  616.3 18.6 %collective-permute-done.13 = bf16[256,2048]{1,0:T(8,128)(2,1)S(1)} collective-permute-done((bf16[256,2048]{1,0:T(8,128)(2,1)S(1)}, bf16[256,2048]{1,0:T(8,128)(2,1)S(1)}, u32[]{:S(2)}, u32[]{:S(2)}) %collective-permute-start.13) | collective-permute-done | bytes 1048608 | tf_op jit(solution)/shard_map/ppermute | solution.py:188
  642.9 6.4 convolution_convert_fusion.4
  649.3 9.9 %collective-permute-start.11 = (bf16[2048,384]{1,0:T(8,128)(2,1)}, bf16[2048,384]{1,0:T(8,128)(2,1)}, u32[]{:S(2)}, u32[]{:S(2)}) collective-permute-start(bf16[2048,384]{1,0:T(8,128)(2,1)} %convolution_convert_fusion.4), channel_id=1, source_target_pairs={{0,1},{3,2},{4,5},{7,6},{8,9},{11,10},{12,13},{15,14},{16,17},{19,... | collective-permute-start | bytes 4718600 | tf_op jit(solution)/shard_map/ppermute | solution.py:188
  670.1 19.9 %collective-permute-start.12 = (bf16[128,2048]{1,0:T(8,128)(2,1)}, bf16[128,2048]{1,0:T(8,128)(2,1)S(1)}, u32[]{:S(2)}, u32[]{:S(2)}) collective-permute-start(bf16[128,2048]{1,0:T(8,128)(2,1)} %reduce-scatter.11.cloned.1.call-done), channel_id=1, source_target_pairs={{0,1},{3,2},{4,5},{7,6},{8,9},{11,10},{12,13},{15,14},{16,17},{19,... | collective-permute-start | bytes 1572872 | tf_op jit(solution)/shard_map/ppermute | solution.py:188
  692.7 7.6 collective-permute-done.12
  715.4 15.5 %collective-permute-done.30 = bf16[256,2048]{1,0:T(8,128)(2,1)} collective-permute-done((bf16[256,2048]{1,0:T(8,128)(2,1)}, bf16[256,2048]{1,0:T(8,128)(2,1)}, u32[]{:S(2)}, u32[]{:S(2)}) %collective-permute-start.30) | collective-permute-done | bytes 1048608 | tf_op jit(solution)/shard_map/ppermute | solution.py:188
  738.5 11.8 %fusion.109 = (f32[2048,1024]{1,0:T(8,128)}, f32[2048,1024]{1,0:T(8,128)}) fusion(bf16[2048,2048]{1,0:T(8,128)(2,1)} %constant_dynamic-update-slice_fusion.5), kind=kLoop, calls=%fused_computation.215 | loop fusion | bytes 33554432 | tf_op jit(solution)/shard_map/slice | solution.py:330
  751.0 16.7 %collective-permute-done.29 = bf16[128,2048]{1,0:T(8,128)(2,1)S(1)} collective-permute-done((bf16[128,2048]{1,0:T(8,128)(2,1)S(1)}, bf16[128,2048]{1,0:T(8,128)(2,1)S(1)}, u32[]{:S(2)}, u32[]{:S(2)}) %collective-permute-start.29) | collective-permute-done | bytes 524320 | tf_op jit(solution)/shard_map/ppermute | solution.py:188
  768.8 29.0 %collective-permute-done.28 = bf16[2048,384]{1,0:T(8,128)(2,1)} collective-permute-done((bf16[2048,384]{1,0:T(8,128)(2,1)}, bf16[2048,384]{1,0:T(8,128)(2,1)}, u32[]{:S(2)}, u32[]{:S(2)}) %collective-permute-start.28) | collective-permute-done | bytes 1572896 | tf_op jit(solution)/shard_map/ppermute | solution.py:188
  803.1 38.3 %psum.7 = f32[4104]{0:T(1024)S(1)} all-reduce(f32[4104]{0:T(1024)S(1)} %pad_maximum_fusion.6), channel_id=1, replica_groups=mesh['heads'=8,'batch'=4] {'heads','batch'}, use_global_device_ids=true, to_apply=%region_23.24 | all-reduce | flops 4104 | bytes 32832 | tf_op jit(solution)/shard_map/psum | solution.py:316
  (376 shorter events, 266.8 us)
Async XLA Ops:
  7.2 59.8 %all-gather.5.cloned.1.call-start = ((), (), s32[]{:S(2)}) async-start(), calls=%async_computation.5 | async-start | bytes 9437184 | tf_op jit(solution)/shard_map/all_gather | solution.py:246
  7.9 97.7 %all-gather.9.cloned.1.call-start = ((), (), s32[]{:S(2)}) async-start(), calls=%async_computation.7 | async-start | bytes 4718592 | tf_op jit(solution)/shard_map/all_gather | solution.py:246
  8.7 136.9 %all-gather.7.cloned.1.call-start = ((), (), s32[]{:S(2)}) async-start(), calls=%async_computation.6 | async-start | bytes 4718592 | tf_op jit(solution)/shard_map/all_gather | solution.py:271
  92.6 109.2 %all-gather.11.cloned.1.call-start = ((), (), s32[]{:S(2)}) async-start(), calls=%async_computation.9 | async-start | bytes 9437184 | tf_op jit(solution)/shard_map/all_gather | solution.py:246
  93.2 243.6 %reduce-scatter.7.cloned.1.call-start = ((), (), s32[]{:S(2)}) async-start(), calls=%async_computation.10 | async-start | bytes 9437184 | tf_op jit(solution)/shard_map/reduce_scatter | solution.py:249
  249.5 147.0 %reduce-scatter.5.cloned.1.call-start = ((), (), s32[]{:S(2)}) async-start(), calls=%async_computation.8 | async-start | bytes 9437184 | tf_op jit(solution)/shard_map/reduce_scatter | solution.py:249
  272.6 53.3 %collective-permute-start.1 = (bf16[256,2048]{1,0:T(8,128)(2,1)S(1)}, bf16[256,2048]{1,0:T(8,128)(2,1)S(1)}, u32[]{:S(2)}, u32[]{:S(2)}) collective-permute-start(bf16[256,2048]{1,0:T(8,128)(2,1)S(1)} %convolution_convert_fusion.13), channel_id=1, source_target_pairs={{0,1},{3,2},{4,5},{7,6},{8,9},{11,10},{12,13},{15,14},{16,17},{19,... | collective-permute-start | bytes 3145736 | tf_op jit(solution)/shard_map/ppermute | solution.py:188
  317.2 97.5 %collective-permute-start.4 = (bf16[256,2048]{1,0:T(8,128)(2,1)}, bf16[256,2048]{1,0:T(8,128)(2,1)}, u32[]{:S(2)}, u32[]{:S(2)}) collective-permute-start(bf16[256,2048]{1,0:T(8,128)(2,1)} %convolution_convert_fusion.11), channel_id=1, source_target_pairs={{0,1},{3,2},{4,5},{7,6},{8,9},{11,10},{12,13},{15,14},{16,17},{19,... | collective-permute-start | bytes 3145736 | tf_op jit(solution)/shard_map/ppermute | solution.py:188
  326.4 93.0 %collective-permute-start.27 = (bf16[256,2048]{1,0:T(8,128)(2,1)S(1)}, bf16[256,2048]{1,0:T(8,128)(2,1)}, u32[]{:S(2)}, u32[]{:S(2)}) collective-permute-start(bf16[256,2048]{1,0:T(8,128)(2,1)S(1)} %add.209), channel_id=1, source_target_pairs={{1,2},{2,1},{5,6},{6,5},{9,10},{10,9},{13,14},{14,13},{17,18},{18,... | collective-permute-start | bytes 3145736 | tf_op jit(solution)/shard_map/ppermute | solution.py:188
  329.4 98.7 %collective-permute-start.26 = (bf16[256,2048]{1,0:T(8,128)(2,1)}, bf16[256,2048]{1,0:T(8,128)(2,1)}, u32[]{:S(2)}, u32[]{:S(2)}) collective-permute-start(bf16[256,2048]{1,0:T(8,128)(2,1)} %add.210), channel_id=1, source_target_pairs={{1,2},{2,1},{5,6},{6,5},{9,10},{10,9},{13,14},{14,13},{17,18},{18,... | collective-permute-start | bytes 3145736 | tf_op jit(solution)/shard_map/ppermute | solution.py:188
  331.0 101.5 %collective-permute-start.3 = (bf16[256,2048]{1,0:T(8,128)(2,1)}, bf16[256,2048]{1,0:T(8,128)(2,1)}, u32[]{:S(2)}, u32[]{:S(2)}) collective-permute-start(bf16[256,2048]{1,0:T(8,128)(2,1)} %convolution_convert_fusion.12), channel_id=1, source_target_pairs={{0,1},{3,2},{4,5},{7,6},{8,9},{11,10},{12,13},{15,14},{16,17},{19,... | collective-permute-start | bytes 3145736 | tf_op jit(solution)/shard_map/ppermute | solution.py:188
  334.4 101.3 %collective-permute-start.2 = (bf16[256,2048]{1,0:T(8,128)(2,1)}, bf16[256,2048]{1,0:T(8,128)(2,1)}, u32[]{:S(2)}, u32[]{:S(2)}) collective-permute-start(bf16[256,2048]{1,0:T(8,128)(2,1)} %convolution_convert_fusion.15), channel_id=1, source_target_pairs={{0,1},{3,2},{4,5},{7,6},{8,9},{11,10},{12,13},{15,14},{16,17},{19,... | collective-permute-start | bytes 3145736 | tf_op jit(solution)/shard_map/ppermute | solution.py:188
  407.5 262.6 %reduce-scatter.11.cloned.1.call-start = ((), (), s32[]{:S(2)}) async-start(), calls=%async_computation.12 | async-start | bytes 4718592 | tf_op jit(solution)/shard_map/reduce_scatter | solution.py:249
  417.7 49.3 %collective-permute-start.25 = (bf16[256,2048]{1,0:T(8,128)(2,1)}, bf16[256,2048]{1,0:T(8,128)(2,1)}, u32[]{:S(2)}, u32[]{:S(2)}) collective-permute-start(bf16[256,2048]{1,0:T(8,128)(2,1)} %add.211), channel_id=1, source_target_pairs={{1,2},{2,1},{5,6},{6,5},{9,10},{10,9},{13,14},{14,13},{17,18},{18,... | collective-permute-start | bytes 3145736 | tf_op jit(solution)/shard_map/ppermute | solution.py:188
  419.3 57.5 %collective-permute-start.7 = (bf16[256,2048]{1,0:T(8,128)(2,1)}, bf16[256,2048]{1,0:T(8,128)(2,1)}, u32[]{:S(2)}, u32[]{:S(2)}) collective-permute-start(bf16[256,2048]{1,0:T(8,128)(2,1)} %convolution_convert_fusion.9), channel_id=1, source_target_pairs={{0,1},{3,2},{4,5},{7,6},{8,9},{11,10},{12,13},{15,14},{16,17},{19,... | collective-permute-start | bytes 3145736 | tf_op jit(solution)/shard_map/ppermute | solution.py:188
  428.1 52.1 %collective-permute-start.41 = (bf16[256,2048]{1,0:T(8,128)(2,1)}, bf16[256,2048]{1,0:T(8,128)(2,1)}, u32[]{:S(2)}, u32[]{:S(2)}) collective-permute-start(bf16[256,2048]{1,0:T(8,128)(2,1)} %add.223), channel_id=1, source_target_pairs={{1,0},{2,3},{5,4},{6,7},{9,8},{10,11},{13,12},{14,15},{17,16},{18,... | collective-permute-start | bytes 3145736 | tf_op jit(solution)/shard_map/ppermute | solution.py:188
  432.5 48.6 %collective-permute-start.40 = (bf16[256,2048]{1,0:T(8,128)(2,1)}, bf16[256,2048]{1,0:T(8,128)(2,1)}, u32[]{:S(2)}, u32[]{:S(2)}) collective-permute-start(bf16[256,2048]{1,0:T(8,128)(2,1)} %add.224), channel_id=1, source_target_pairs={{1,0},{2,3},{5,4},{6,7},{9,8},{10,11},{13,12},{14,15},{17,16},{18,... | collective-permute-start | bytes 3145736 | tf_op jit(solution)/shard_map/ppermute | solution.py:188
  435.7 56.8 %collective-permute-start.24 = (bf16[256,2048]{1,0:T(8,128)(2,1)S(1)}, bf16[256,2048]{1,0:T(8,128)(2,1)}, u32[]{:S(2)}, u32[]{:S(2)}) collective-permute-start(bf16[256,2048]{1,0:T(8,128)(2,1)S(1)} %add.212), channel_id=1, source_target_pairs={{1,2},{2,1},{5,6},{6,5},{9,10},{10,9},{13,14},{14,13},{17,18},{18,... | collective-permute-start | bytes 3145736 | tf_op jit(solution)/shard_map/ppermute | solution.py:188
  444.7 356.5 %reduce-scatter.9.cloned.1.call-start = ((), (), s32[]{:S(2)}) async-start(), calls=%async_computation.11 | async-start | bytes 9437184 | tf_op jit(solution)/shard_map/reduce_scatter | solution.py:249
  492.5 46.0 %collective-permute-start.5 = (bf16[256,2048]{1,0:T(8,128)(2,1)S(1)}, bf16[256,2048]{1,0:T(8,128)(2,1)S(1)}, u32[]{:S(2)}, u32[]{:S(2)}) collective-permute-start(bf16[256,2048]{1,0:T(8,128)(2,1)S(1)} %copy-done.21), channel_id=1, source_target_pairs={{0,1},{3,2},{4,5},{7,6},{8,9},{11,10},{12,13},{15,14},{16,17},{19,... | collective-permute-start | bytes 3145736 | tf_op jit(solution)/shard_map/ppermute | solution.py:188
  498.8 60.2 %collective-permute-start.10 = (bf16[256,2048]{1,0:T(8,128)(2,1)S(1)}, bf16[256,2048]{1,0:T(8,128)(2,1)S(1)}, u32[]{:S(2)}, u32[]{:S(2)}) collective-permute-start(bf16[256,2048]{1,0:T(8,128)(2,1)S(1)} %copy-done.19), channel_id=1, source_target_pairs={{0,1},{3,2},{4,5},{7,6},{8,9},{11,10},{12,13},{15,14},{16,17},{19,... | collective-permute-start | bytes 3145736 | tf_op jit(solution)/shard_map/ppermute | solution.py:188
  506.1 54.2 %collective-permute-start.38 = (bf16[256,2048]{1,0:T(8,128)(2,1)S(1)}, bf16[256,2048]{1,0:T(8,128)(2,1)S(1)}, u32[]{:S(2)}, u32[]{:S(2)}) collective-permute-start(bf16[256,2048]{1,0:T(8,128)(2,1)S(1)} %add.226), channel_id=1, source_target_pairs={{1,0},{2,3},{5,4},{6,7},{9,8},{10,11},{13,12},{14,15},{17,16},{18,... | collective-permute-start | bytes 3145736 | tf_op jit(solution)/shard_map/ppermute | solution.py:188
  516.0 53.7 %collective-permute-start.37 = (bf16[256,2048]{1,0:T(8,128)(2,1)S(1)}, bf16[256,2048]{1,0:T(8,128)(2,1)S(1)}, u32[]{:S(2)}, u32[]{:S(2)}) collective-permute-start(bf16[256,2048]{1,0:T(8,128)(2,1)S(1)} %add.227), channel_id=1, source_target_pairs={{1,0},{2,3},{5,4},{6,7},{9,8},{10,11},{13,12},{14,15},{17,16},{18,... | collective-permute-start | bytes 3145736 | tf_op jit(solution)/shard_map/ppermute | solution.py:188
  518.1 72.0 %collective-permute-start.36 = (bf16[256,2048]{1,0:T(8,128)(2,1)S(1)}, bf16[256,2048]{1,0:T(8,128)(2,1)S(1)}, u32[]{:S(2)}, u32[]{:S(2)}) collective-permute-start(bf16[256,2048]{1,0:T(8,128)(2,1)S(1)} %add.228), channel_id=1, source_target_pairs={{1,0},{2,3},{5,4},{6,7},{9,8},{10,11},{13,12},{14,15},{17,16},{18,... | collective-permute-start | bytes 3145736 | tf_op jit(solution)/shard_map/ppermute | solution.py:188
  538.5 53.2 %collective-permute-start.21 = (bf16[256,2048]{1,0:T(8,128)(2,1)S(1)}, bf16[256,2048]{1,0:T(8,128)(2,1)S(1)}, u32[]{:S(2)}, u32[]{:S(2)}) collective-permute-start(bf16[256,2048]{1,0:T(8,128)(2,1)S(1)} %add.215), channel_id=1, source_target_pairs={{1,2},{2,1},{5,6},{6,5},{9,10},{10,9},{13,14},{14,13},{17,18},{18,... | collective-permute-start | bytes 3145736 | tf_op jit(solution)/shard_map/ppermute | solution.py:188
  593.6 48.6 %collective-permute-start.35 = (bf16[256,2048]{1,0:T(8,128)(2,1)S(1)}, bf16[256,2048]{1,0:T(8,128)(2,1)S(1)}, u32[]{:S(2)}, u32[]{:S(2)}) collective-permute-start(bf16[256,2048]{1,0:T(8,128)(2,1)S(1)} %add.229), channel_id=1, source_target_pairs={{1,0},{2,3},{5,4},{6,7},{9,8},{10,11},{13,12},{14,15},{17,16},{18,... | collective-permute-start | bytes 3145736 | tf_op jit(solution)/shard_map/ppermute | solution.py:188
  596.8 52.5 %collective-permute-start.34 = (bf16[256,2048]{1,0:T(8,128)(2,1)S(1)}, bf16[256,2048]{1,0:T(8,128)(2,1)S(1)}, u32[]{:S(2)}, u32[]{:S(2)}) collective-permute-start(bf16[256,2048]{1,0:T(8,128)(2,1)S(1)} %add.230), channel_id=1, source_target_pairs={{1,0},{2,3},{5,4},{6,7},{9,8},{10,11},{13,12},{14,15},{17,16},{18,... | collective-permute-start | bytes 3145736 | tf_op jit(solution)/shard_map/ppermute | solution.py:188
  598.5 66.2 %collective-permute-start.33 = (bf16[256,2048]{1,0:T(8,128)(2,1)S(1)}, bf16[256,2048]{1,0:T(8,128)(2,1)S(1)}, u32[]{:S(2)}, u32[]{:S(2)}) collective-permute-start(bf16[256,2048]{1,0:T(8,128)(2,1)S(1)} %add.231), channel_id=1, source_target_pairs={{1,0},{2,3},{5,4},{6,7},{9,8},{10,11},{13,12},{14,15},{17,16},{18,... | collective-permute-start | bytes 3145736 | tf_op jit(solution)/shard_map/ppermute | solution.py:188
  649.3 52.1 %collective-permute-start.11 = (bf16[2048,384]{1,0:T(8,128)(2,1)}, bf16[2048,384]{1,0:T(8,128)(2,1)}, u32[]{:S(2)}, u32[]{:S(2)}) collective-permute-start(bf16[2048,384]{1,0:T(8,128)(2,1)} %convolution_convert_fusion.4), channel_id=1, source_target_pairs={{0,1},{3,2},{4,5},{7,6},{8,9},{11,10},{12,13},{15,14},{16,17},{19,... | collective-permute-start | bytes 4718600 | tf_op jit(solution)/shard_map/ppermute | solution.py:188
  666.1 46.7 %collective-permute-start.31 = (bf16[256,2048]{1,0:T(8,128)(2,1)}, bf16[256,2048]{1,0:T(8,128)(2,1)}, u32[]{:S(2)}, u32[]{:S(2)}) collective-permute-start(bf16[256,2048]{1,0:T(8,128)(2,1)} %add.233), channel_id=1, source_target_pairs={{1,0},{2,3},{5,4},{6,7},{9,8},{10,11},{13,12},{14,15},{17,16},{18,... | collective-permute-start | bytes 3145736 | tf_op jit(solution)/shard_map/ppermute | solution.py:188
  668.8 62.1 %collective-permute-start.30 = (bf16[256,2048]{1,0:T(8,128)(2,1)}, bf16[256,2048]{1,0:T(8,128)(2,1)}, u32[]{:S(2)}, u32[]{:S(2)}) collective-permute-start(bf16[256,2048]{1,0:T(8,128)(2,1)} %add.234), channel_id=1, source_target_pairs={{1,0},{2,3},{5,4},{6,7},{9,8},{10,11},{13,12},{14,15},{17,16},{18,... | collective-permute-start | bytes 3145736 | tf_op jit(solution)/shard_map/ppermute | solution.py:188
  737.2 60.6 %collective-permute-start.28 = (bf16[2048,384]{1,0:T(8,128)(2,1)}, bf16[2048,384]{1,0:T(8,128)(2,1)}, u32[]{:S(2)}, u32[]{:S(2)}) collective-permute-start(bf16[2048,384]{1,0:T(8,128)(2,1)} %add.236), channel_id=1, source_target_pairs={{1,0},{2,3},{5,4},{6,7},{9,8},{10,11},{13,12},{14,15},{17,16},{18,... | collective-permute-start | bytes 4718600 | tf_op jit(solution)/shard_map/ppermute | solution.py:188
  (92 other events, 1406.5 us)
Sparse Core Ops, SparseCore 0:
  9.9 57.0 all-gather.4
  68.9 36.7 all-gather.8
  108.1 37.4 all-gather.6
  147.3 54.3 all-gather.10
  249.7 71.2 reduce-scatter.6
  325.2 71.2 reduce-scatter.4
  444.8 55.6 reduce-scatter.10
  504.3 71.2 reduce-scatter.8
where the time goes:
time: 862 us; the launch traced here: 853 us
  waiting for transfers between devices  344 us (40%)
  matrix products  207 us (24%)
  starting transfers between devices  109 us (13%)
  other arithmetic  95.5 us (11%)
  local copies, waits for them, and re-layouts  41.4 us (5%)
  blocking collectives  38.3 us (4%)
  between operations  17.7 us (2%)
    ppermute x42, waiting for transfers between devices, add(): arrived = lax.ppermute(array, self.axis, pairs)  182 us
    ppermute x42, starting transfers between devices, add(): arrived = lax.ppermute(array, self.axis, pairs)  104 us
    dot_general x14, matrix products, dot_cols(): lax.dot_general(left_mat, right_mat, (((0,), (0,)), ((), ())), preferred_...  78.3 us
    all_gather x3, waiting for transfers between devices, gather(): return lax.all_gather(array, 'heads', axis=0, tiled=True)  64.1 us
    reduce_scatter x4, waiting for transfers between devices, scatter(): return lax.psum_scatter(array, 'heads', scatter_dimension=0, tiled=True)  56.7 us
    dot_general x4, matrix products, dot_rows(): lax.dot_general(left_mat, right_mat, (((1,), (1,)), ((), ())), preferred_...  53.9 us
    all_gather x1, waiting for transfers between devices, per_device(): mixed_all = lax.all_gather(mixed, 'heads', axis=1, tiled=True)  39.9 us
    psum x1, blocking collectives, per_device(): lax.psum(jnp.concatenate([gain_attn_part, gain_mlp_part, slots]), ('heads...  38.3 us
  transfers between devices with their start and end apart: 51, of which 17 were waited for; matrix products, arithmetic and copies ran while one was open for 33% of the time, Pallas kernels for 0%

commit v1 on v0

--- a/solution.py
+++ b/solution.py
@@ -10,6 +10,28 @@
 MICRO = 2
 epsilon = 1e-05
 big_negative = -1e30
+
+
+def joined_along(blocks, dim):
+    shape = list(blocks.shape[1:])
+    shape[dim] *= blocks.shape[0]
+    return jnp.moveaxis(blocks, 0, dim).reshape(shape)
+
+
+def ring_gather(array, axis, dim):
+    count = lax.axis_size(axis)
+    pairs = [(i, (i + 1) % count) for i in range(count)]
+    back = [(b, a) for a, b in pairs]
+    lower, upper = ([], [])
+    for step in range(count - 1):
+        if step % 2 == 0:
+            lower.append(lax.ppermute(lower[-1] if lower else array, axis, pairs))
+        else:
+            upper.append(lax.ppermute(upper[-1] if upper else array, axis, back))
+    pieces = jnp.stack([*lower[::-1], array, *upper])
+    shift = lax.axis_index(axis) - len(lower)
+    pieces = pieces[(jnp.arange(count) - shift) % count]
+    return joined_along(pieces, dim)
 
 
 def dot_rows(left_mat, right_mat):
@@ -268,7 +290,7 @@
     query, key, value = [by_sequence(qkv[:, i * DH : (i + 1) * DH]) for i in range(3)]
     head_kept = head_forward(query, key, value, share, positions, doc_ids, valid_keys)
     mixed = by_device(head_kept[0].astype(low))
-    mixed_all = lax.all_gather(mixed, "heads", axis=1, tiled=True)
+    mixed_all = ring_gather(mixed, "heads", 1)
     cot_all = gather(cot_own)
     y1_all = x_all + jnp.dot(mixed_all, w_out_all, preferred_element_type=jnp.float32)
     h2_all = (y1_all * norm_scale(y1_all) * norm_mlp).astype(low)

time: 862 us -> 901 us (1.045)
  local copies, waits for them, and re-layouts: 41.4 us -> 56.7 us
  waiting for transfers between devices: 344 us -> 359 us
    ppermute x0 -> x7, waiting for transfers between devices: none -> 66.2 us  [the longest x4 66.2 us: ring_gather(): lower.append(lax.ppermute(lower[-1] if lower else array, axis, pairs))]
    all_gather x1 -> x0, waiting for transfers between devices: 39.9 us -> none  [per_device(): mixed_all = lax.all_gather(mixed, 'heads', axis=1, tiled=True)]
    all_gather x3, waiting for transfers between devices: 64.1 us -> 52.2 us  [gather(): return lax.all_gather(array, 'heads', axis=0, tiled=True)]
    unnamed x150 -> x161, local copies, waits for them, and re-layouts: 20.8 us -> 26.1 us
  transfers between devices with their start and end apart: 51 -> 57, of which waited for: 17 -> 18; matrix products, arithmetic and copies ran while one was open for 33% -> 33% of each run, Pallas kernels for 0% -> 0%
where the time goes in v1:
time: 901 us; the launch traced here: 892 us
  waiting for transfers between devices  359 us (40%)
  matrix products  208 us (23%)
  starting transfers between devices  117 us (13%)
  other arithmetic  95.4 us (11%)
  local copies, waits for them, and re-layouts  56.7 us (6%)
  blocking collectives  38.6 us (4%)
  between operations  17.8 us (2%)
    ppermute x42, waiting for transfers between devices, add(): arrived = lax.ppermute(array, self.axis, pairs)  182 us
    ppermute x42, starting transfers between devices, add(): arrived = lax.ppermute(array, self.axis, pairs)  104 us
    dot_general x14, matrix products, dot_cols(): lax.dot_general(left_mat, right_mat, (((0,), (0,)), ((), ())), preferred_...  77.9 us
    ppermute x4, waiting for transfers between devices, ring_gather(): lower.append(lax.ppermute(lower[-1] if lower else array, axis, pairs))  66.2 us
    reduce_scatter x4, waiting for transfers between devices, scatter(): return lax.psum_scatter(array, 'heads', scatter_dimension=0, tiled=True)  56.4 us
    dot_general x4, matrix products, dot_rows(): lax.dot_general(left_mat, right_mat, (((1,), (1,)), ((), ())), preferred_...  53.8 us
    all_gather x3, waiting for transfers between devices, gather(): return lax.all_gather(array, 'heads', axis=0, tiled=True)  52.2 us
    psum x1, blocking collectives, per_device(): lax.psum(jnp.concatenate([gain_attn_part, gain_mlp_part, slots]), ('heads...  38.6 us
  transfers between devices with their start and end apart: 57, of which 18 were waited for; matrix products, arithmetic and copies ran while one was open for 33% of the time, Pallas kernels for 0%

profile of v1, /device:TPU:0, one launch (start us, length us, event | category | flops | bytes accessed | tf_op | source)
XLA Modules:
  0.0 891.8 jit_solution(17749934055492586856)
XLA Ops:
  14.9 52.2 %all-gather.4.cloned.1.call-done = bf16[2048,2048]{1,0:T(8,128)(2,1)} async-done(((bf16[256,2048]{1,0:T(8,128)(2,1)}), bf16[2048,2048]{1,0:T(8,128)(2,1)}) %all-gather.4.cloned.1.call-update) | async-done | bytes 8388624 | tf_op jit(solution)/shard_map/all_gather | solution.py:268
  92.2 18.3 %collective-permute-done = bf16[2048,128]{1,0:T(8,128)(2,1)S(1)} collective-permute-done((bf16[2048,128]{1,0:T(8,128)(2,1)S(1)}, bf16[2048,128]{1,0:T(8,128)(2,1)S(1)}, u32[]{:S(2)}, u32[]{:S(2)}) %collective-permute-start) | collective-permute-done | bytes 524320 | tf_op jit(solution)/shard_map/ppermute | solution.py:28
  113.1 14.4 %collective-permute-done.1 = bf16[2048,128]{1,0:T(8,128)(2,1)S(1)} collective-permute-done((bf16[2048,128]{1,0:T(8,128)(2,1)S(1)}, bf16[2048,128]{1,0:T(8,128)(2,1)S(1)}, u32[]{:S(2)}, u32[]{:S(2)}) %collective-permute-start.1) | collective-permute-done | bytes 524320 | tf_op jit(solution)/shard_map/ppermute | solution.py:28
  133.1 14.9 %collective-permute-done.2 = bf16[2048,128]{1,0:T(8,128)(2,1)S(1)} collective-permute-done((bf16[2048,128]{1,0:T(8,128)(2,1)S(1)}, bf16[2048,128]{1,0:T(8,128)(2,1)S(1)}, u32[]{:S(2)}, u32[]{:S(2)}) %collective-permute-start.2) | collective-permute-done | bytes 524320 | tf_op jit(solution)/shard_map/ppermute | solution.py:28
  154.7 18.6 %collective-permute-done.3 = bf16[2048,128]{1,0:T(8,128)(2,1)S(1)} collective-permute-done((bf16[2048,128]{1,0:T(8,128)(2,1)S(1)}, bf16[2048,128]{1,0:T(8,128)(2,1)S(1)}, u32[]{:S(2)}, u32[]{:S(2)}) %collective-permute-start.3) | collective-permute-done | bytes 524320 | tf_op jit(solution)/shard_map/ppermute | solution.py:28
  185.2 6.7 copy.64
  191.9 14.8 %multiply_reduce_fusion = (f32[2048]{0:T(1024)S(1)}, f32[2048,2048]{1,0:T(8,128)S(1)}) fusion(bf16[2048,1024]{0,1:T(8,128)(2,1)} %bitcast.135, bf16[1024,2048]{1,0:T(8,128)(2,1)} %all-gather.6.cloned.1.call-done, bf16[2048,2048]{1,0:T(8,128)(2,1)} %all-gather.4.cloned.1.call-done), kind=kOutput, calls=%fused_computation.10 | convolution fusion | flops 8606709760 | bytes 33562624 | tf_op jit(solution)/shard_map/dot_general | solution.py:295
  217.0 24.3 %fusion.127 = f32[2048,2048]{0,1:T(8,128)} fusion(bf16[2048,2048]{1,0:T(8,128)(2,1)} %multiply_convert_fusion, bf16[2048,2048]{1,0:T(8,128)(2,1)} %copy-done.14), kind=kOutput, calls=%fused_computation.239 | convolution fusion | flops 17179869184 | bytes 33554432 | tf_op jit(solution)/shard_map/dot_general | solution.py:299
  241.3 22.8 %multiply_convert_fusion.2 = (bf16[2048,1024]{0,1:T(8,128)(2,1)S(1)}, bf16[2048,1024]{0,1:T(8,128)(2,1)}, bf16[2048,1024]{0,1:T(8,128)(2,1)}) fusion(f32[2048,2048]{0,1:T(8,128)} %fusion.127, bf16[2048,2048]{1,0:T(8,128)(2,1)} %all-gather.8.cloned.1.call-done, bf16[1024,2048]{1,0:T(8,128)(2,1)} %param.24), kind=kOutput, calls=%fused_computation.13 | convolution fusion | flops 8623489024 | bytes 41943040 | tf_op jit(solution)/shard_map/dot_general | solution.py:38
  266.1 22.9 %convolution_convert_fusion.1 = bf16[2048,2048]{1,0:T(8,128)(2,1)} fusion(bf16[2048,2048]{1,0:T(8,128)(2,1)} %copy-done.14, bf16[2048,1024]{0,1:T(8,128)(2,1)} %get-tuple-element.249, bf16[2048,1024]{0,1:T(8,128)(2,1)S(1)} %get-tuple-element.248), kind=kOutput, calls=%fused_computation.17 | convolution fusion | flops 17200840704 | bytes 25165824 | tf_op jit(solution)/shard_map/dot_general | solution.py:38
  289.1 14.5 %convolution_convert_fusion.2 = bf16[2048,2048]{1,0:T(8,128)(2,1)} fusion(bf16[2048,1024]{0,1:T(8,128)(2,1)} %get-tuple-element.252, bf16[1024,2048]{1,0:T(8,128)(2,1)} %param.24), kind=kOutput, calls=%fused_computation.18 | convolution fusion | flops 8594128896 | bytes 16777216 | tf_op jit(solution)/shard_map/dot_general | solution.py:319
  337.0 7.1 convolution_convert_fusion.16
  348.9 7.2 convolution_convert_fusion.7
  378.8 56.3 %reduce-scatter.5.cloned.1.call-done = bf16[256,2048]{1,0:T(8,128)(2,1)} async-done(((bf16[2048,2048]{1,0:T(8,128)(2,1)}), bf16[256,2048]{1,0:T(8,128)(2,1)}) %reduce-scatter.5.cloned.1.call-update) | async-done | bytes 1048592 | tf_op jit(solution)/shard_map/reduce_scatter | solution.py:271
  446.1 7.1 convolution_convert_fusion.8
  498.7 6.8 convolution_convert_fusion
  519.2 11.7 %collective-permute-start.13 = (bf16[256,2048]{1,0:T(8,128)(2,1)S(1)}, bf16[256,2048]{1,0:T(8,128)(2,1)S(1)}, u32[]{:S(2)}, u32[]{:S(2)}) collective-permute-start(bf16[256,2048]{1,0:T(8,128)(2,1)S(1)} %copy-done.24), channel_id=1, source_target_pairs={{0,1},{3,2},{4,5},{7,6},{8,9},{11,10},{12,13},{15,14},{16,17},{19,... | collective-permute-start | bytes 3145736 | tf_op jit(solution)/shard_map/ppermute | solution.py:210
  545.6 8.8 collective-permute-done.13
  557.8 19.1 %collective-permute-done.12 = bf16[256,2048]{1,0:T(8,128)(2,1)S(1)} collective-permute-done((bf16[256,2048]{1,0:T(8,128)(2,1)S(1)}, bf16[256,2048]{1,0:T(8,128)(2,1)S(1)}, u32[]{:S(2)}, u32[]{:S(2)}) %collective-permute-start.12) | collective-permute-done | bytes 1048608 | tf_op jit(solution)/shard_map/ppermute | solution.py:210
  579.4 18.0 %collective-permute-done.17 = bf16[256,2048]{1,0:T(8,128)(2,1)S(1)} collective-permute-done((bf16[256,2048]{1,0:T(8,128)(2,1)S(1)}, bf16[256,2048]{1,0:T(8,128)(2,1)S(1)}, u32[]{:S(2)}, u32[]{:S(2)}) %collective-permute-start.17) | collective-permute-done | bytes 1048608 | tf_op jit(solution)/shard_map/ppermute | solution.py:210
  599.4 8.5 collective-permute-done.44
  609.4 18.9 %collective-permute-done.43 = bf16[256,2048]{1,0:T(8,128)(2,1)S(1)} collective-permute-done((bf16[256,2048]{1,0:T(8,128)(2,1)S(1)}, bf16[256,2048]{1,0:T(8,128)(2,1)S(1)}, u32[]{:S(2)}, u32[]{:S(2)}) %collective-permute-start.43) | collective-permute-done | bytes 1048608 | tf_op jit(solution)/shard_map/ppermute | solution.py:210
  638.4 14.9 %collective-permute-done.15 = bf16[256,2048]{1,0:T(8,128)(2,1)S(1)} collective-permute-done((bf16[256,2048]{1,0:T(8,128)(2,1)S(1)}, bf16[256,2048]{1,0:T(8,128)(2,1)S(1)}, u32[]{:S(2)}, u32[]{:S(2)}) %collective-permute-start.15) | collective-permute-done | bytes 1048608 | tf_op jit(solution)/shard_map/ppermute | solution.py:210
  654.5 18.7 %collective-permute-done.20 = bf16[256,2048]{1,0:T(8,128)(2,1)S(1)} collective-permute-done((bf16[256,2048]{1,0:T(8,128)(2,1)S(1)}, bf16[256,2048]{1,0:T(8,128)(2,1)S(1)}, u32[]{:S(2)}, u32[]{:S(2)}) %collective-permute-start.20) | collective-permute-done | bytes 1048608 | tf_op jit(solution)/shard_map/ppermute | solution.py:210
  687.6 10.0 %collective-permute-start.18 = (bf16[2048,384]{1,0:T(8,128)(2,1)}, bf16[2048,384]{1,0:T(8,128)(2,1)}, u32[]{:S(2)}, u32[]{:S(2)}) collective-permute-start(bf16[2048,384]{1,0:T(8,128)(2,1)} %convolution_convert_fusion.4), channel_id=1, source_target_pairs={{0,1},{3,2},{4,5},{7,6},{8,9},{11,10},{12,13},{15,14},{16,17},{19,... | collective-permute-start | bytes 4718600 | tf_op jit(solution)/shard_map/ppermute | solution.py:210
  708.4 20.1 %collective-permute-start.19 = (bf16[128,2048]{1,0:T(8,128)(2,1)}, bf16[128,2048]{1,0:T(8,128)(2,1)S(1)}, u32[]{:S(2)}, u32[]{:S(2)}) collective-permute-start(bf16[128,2048]{1,0:T(8,128)(2,1)} %reduce-scatter.11.cloned.1.call-done), channel_id=1, source_target_pairs={{0,1},{3,2},{4,5},{7,6},{8,9},{11,10},{12,13},{15,14},{16,17},{19,... | collective-permute-start | bytes 1572872 | tf_op jit(solution)/shard_map/ppermute | solution.py:210
  731.1 7.6 collective-permute-done.19
  753.7 15.5 %collective-permute-done.37 = bf16[256,2048]{1,0:T(8,128)(2,1)} collective-permute-done((bf16[256,2048]{1,0:T(8,128)(2,1)}, bf16[256,2048]{1,0:T(8,128)(2,1)}, u32[]{:S(2)}, u32[]{:S(2)}) %collective-permute-start.37) | collective-permute-done | bytes 1048608 | tf_op jit(solution)/shard_map/ppermute | solution.py:210
  776.8 11.8 %fusion.111 = (f32[2048,1024]{1,0:T(8,128)}, f32[2048,1024]{1,0:T(8,128)}) fusion(bf16[2048,2048]{1,0:T(8,128)(2,1)} %constant_dynamic-update-slice_fusion.6), kind=kLoop, calls=%fused_computation.231 | loop fusion | bytes 33554432 | tf_op jit(solution)/shard_map/slice | solution.py:352
  789.1 17.0 %collective-permute-done.36 = bf16[128,2048]{1,0:T(8,128)(2,1)S(1)} collective-permute-done((bf16[128,2048]{1,0:T(8,128)(2,1)S(1)}, bf16[128,2048]{1,0:T(8,128)(2,1)S(1)}, u32[]{:S(2)}, u32[]{:S(2)}) %collective-permute-start.36) | collective-permute-done | bytes 524320 | tf_op jit(solution)/shard_map/ppermute | solution.py:210
  807.2 29.0 %collective-permute-done.35 = bf16[2048,384]{1,0:T(8,128)(2,1)} collective-permute-done((bf16[2048,384]{1,0:T(8,128)(2,1)}, bf16[2048,384]{1,0:T(8,128)(2,1)}, u32[]{:S(2)}, u32[]{:S(2)}) %collective-permute-start.35) | collective-permute-done | bytes 1572896 | tf_op jit(solution)/shard_map/ppermute | solution.py:210
  841.5 38.6 %psum.7 = f32[4104]{0:T(1024)S(1)} all-reduce(f32[4104]{0:T(1024)S(1)} %pad_maximum_fusion.6), channel_id=1, replica_groups=mesh['heads'=8,'batch'=4] {'heads','batch'}, use_global_device_ids=true, to_apply=%region_23.24 | all-reduce | flops 4104 | bytes 32832 | tf_op jit(solution)/shard_map/psum | solution.py:338
  (403 shorter events, 296.7 us)
Async XLA Ops:
  7.2 59.8 %all-gather.4.cloned.1.call-start = ((), (), s32[]{:S(2)}) async-start(), calls=%async_computation.5 | async-start | bytes 9437184 | tf_op jit(solution)/shard_map/all_gather | solution.py:268
  7.9 184.0 %all-gather.6.cloned.1.call-start = ((), (), s32[]{:S(2)}) async-start(), calls=%async_computation.6 | async-start | bytes 4718592 | tf_op jit(solution)/shard_map/all_gather | solution.py:268
  8.7 232.6 %all-gather.8.cloned.1.call-start = ((), (), s32[]{:S(2)}) async-start(), calls=%async_computation.8 | async-start | bytes 9437184 | tf_op jit(solution)/shard_map/all_gather | solution.py:268
  9.4 366.2 %reduce-scatter.7.cloned.1.call-start = ((), (), s32[]{:S(2)}) async-start(), calls=%async_computation.9 | async-start | bytes 9437184 | tf_op jit(solution)/shard_map/reduce_scatter | solution.py:271
  289.0 146.1 %reduce-scatter.5.cloned.1.call-start = ((), (), s32[]{:S(2)}) async-start(), calls=%async_computation.7 | async-start | bytes 9437184 | tf_op jit(solution)/shard_map/reduce_scatter | solution.py:271
  311.9 52.9 %collective-permute-start.8 = (bf16[256,2048]{1,0:T(8,128)(2,1)S(1)}, bf16[256,2048]{1,0:T(8,128)(2,1)S(1)}, u32[]{:S(2)}, u32[]{:S(2)}) collective-permute-start(bf16[256,2048]{1,0:T(8,128)(2,1)S(1)} %convolution_convert_fusion.13), channel_id=1, source_target_pairs={{0,1},{3,2},{4,5},{7,6},{8,9},{11,10},{12,13},{15,14},{16,17},{19,... | collective-permute-start | bytes 3145736 | tf_op jit(solution)/shard_map/ppermute | solution.py:210
  356.1 97.1 %collective-permute-start.11 = (bf16[256,2048]{1,0:T(8,128)(2,1)}, bf16[256,2048]{1,0:T(8,128)(2,1)}, u32[]{:S(2)}, u32[]{:S(2)}) collective-permute-start(bf16[256,2048]{1,0:T(8,128)(2,1)} %convolution_convert_fusion.11), channel_id=1, source_target_pairs={{0,1},{3,2},{4,5},{7,6},{8,9},{11,10},{12,13},{15,14},{16,17},{19,... | collective-permute-start | bytes 3145736 | tf_op jit(solution)/shard_map/ppermute | solution.py:210
  365.3 92.5 %collective-permute-start.34 = (bf16[256,2048]{1,0:T(8,128)(2,1)S(1)}, bf16[256,2048]{1,0:T(8,128)(2,1)}, u32[]{:S(2)}, u32[]{:S(2)}) collective-permute-start(bf16[256,2048]{1,0:T(8,128)(2,1)S(1)} %add.235), channel_id=1, source_target_pairs={{1,2},{2,1},{5,6},{6,5},{9,10},{10,9},{13,14},{14,13},{17,18},{18,... | collective-permute-start | bytes 3145736 | tf_op jit(solution)/shard_map/ppermute | solution.py:210
  368.3 98.2 %collective-permute-start.33 = (bf16[256,2048]{1,0:T(8,128)(2,1)}, bf16[256,2048]{1,0:T(8,128)(2,1)}, u32[]{:S(2)}, u32[]{:S(2)}) collective-permute-start(bf16[256,2048]{1,0:T(8,128)(2,1)} %add.236), channel_id=1, source_target_pairs={{1,2},{2,1},{5,6},{6,5},{9,10},{10,9},{13,14},{14,13},{17,18},{18,... | collective-permute-start | bytes 3145736 | tf_op jit(solution)/shard_map/ppermute | solution.py:210
  370.0 101.2 %collective-permute-start.10 = (bf16[256,2048]{1,0:T(8,128)(2,1)}, bf16[256,2048]{1,0:T(8,128)(2,1)}, u32[]{:S(2)}, u32[]{:S(2)}) collective-permute-start(bf16[256,2048]{1,0:T(8,128)(2,1)} %convolution_convert_fusion.12), channel_id=1, source_target_pairs={{0,1},{3,2},{4,5},{7,6},{8,9},{11,10},{12,13},{15,14},{16,17},{19,... | collective-permute-start | bytes 3145736 | tf_op jit(solution)/shard_map/ppermute | solution.py:210
  373.3 101.1 %collective-permute-start.9 = (bf16[256,2048]{1,0:T(8,128)(2,1)}, bf16[256,2048]{1,0:T(8,128)(2,1)}, u32[]{:S(2)}, u32[]{:S(2)}) collective-permute-start(bf16[256,2048]{1,0:T(8,128)(2,1)} %convolution_convert_fusion.15), channel_id=1, source_target_pairs={{0,1},{3,2},{4,5},{7,6},{8,9},{11,10},{12,13},{15,14},{16,17},{19,... | collective-permute-start | bytes 3145736 | tf_op jit(solution)/shard_map/ppermute | solution.py:210
  446.0 262.3 %reduce-scatter.11.cloned.1.call-start = ((), (), s32[]{:S(2)}) async-start(), calls=%async_computation.11 | async-start | bytes 4718592 | tf_op jit(solution)/shard_map/reduce_scatter | solution.py:271
  456.2 49.4 %collective-permute-start.32 = (bf16[256,2048]{1,0:T(8,128)(2,1)}, bf16[256,2048]{1,0:T(8,128)(2,1)}, u32[]{:S(2)}, u32[]{:S(2)}) collective-permute-start(bf16[256,2048]{1,0:T(8,128)(2,1)} %add.237), channel_id=1, source_target_pairs={{1,2},{2,1},{5,6},{6,5},{9,10},{10,9},{13,14},{14,13},{17,18},{18,... | collective-permute-start | bytes 3145736 | tf_op jit(solution)/shard_map/ppermute | solution.py:210
  457.8 57.0 %collective-permute-start.14 = (bf16[256,2048]{1,0:T(8,128)(2,1)}, bf16[256,2048]{1,0:T(8,128)(2,1)}, u32[]{:S(2)}, u32[]{:S(2)}) collective-permute-start(bf16[256,2048]{1,0:T(8,128)(2,1)} %convolution_convert_fusion.9), channel_id=1, source_target_pairs={{0,1},{3,2},{4,5},{7,6},{8,9},{11,10},{12,13},{15,14},{16,17},{19,... | collective-permute-start | bytes 3145736 | tf_op jit(solution)/shard_map/ppermute | solution.py:210
  466.6 51.7 %collective-permute-start.48 = (bf16[256,2048]{1,0:T(8,128)(2,1)}, bf16[256,2048]{1,0:T(8,128)(2,1)}, u32[]{:S(2)}, u32[]{:S(2)}) collective-permute-start(bf16[256,2048]{1,0:T(8,128)(2,1)} %add.249), channel_id=1, source_target_pairs={{1,0},{2,3},{5,4},{6,7},{9,8},{10,11},{13,12},{14,15},{17,16},{18,... | collective-permute-start | bytes 3145736 | tf_op jit(solution)/shard_map/ppermute | solution.py:210
  471.2 48.0 %collective-permute-start.47 = (bf16[256,2048]{1,0:T(8,128)(2,1)}, bf16[256,2048]{1,0:T(8,128)(2,1)}, u32[]{:S(2)}, u32[]{:S(2)}) collective-permute-start(bf16[256,2048]{1,0:T(8,128)(2,1)} %add.250), channel_id=1, source_target_pairs={{1,0},{2,3},{5,4},{6,7},{9,8},{10,11},{13,12},{14,15},{17,16},{18,... | collective-permute-start | bytes 3145736 | tf_op jit(solution)/shard_map/ppermute | solution.py:210
  474.4 56.5 %collective-permute-start.31 = (bf16[256,2048]{1,0:T(8,128)(2,1)S(1)}, bf16[256,2048]{1,0:T(8,128)(2,1)}, u32[]{:S(2)}, u32[]{:S(2)}) collective-permute-start(bf16[256,2048]{1,0:T(8,128)(2,1)S(1)} %add.238), channel_id=1, source_target_pairs={{1,2},{2,1},{5,6},{6,5},{9,10},{10,9},{13,14},{14,13},{17,18},{18,... | collective-permute-start | bytes 3145736 | tf_op jit(solution)/shard_map/ppermute | solution.py:210
  483.3 356.2 %reduce-scatter.9.cloned.1.call-start = ((), (), s32[]{:S(2)}) async-start(), calls=%async_computation.10 | async-start | bytes 9437184 | tf_op jit(solution)/shard_map/reduce_scatter | solution.py:271
  530.9 46.0 %collective-permute-start.12 = (bf16[256,2048]{1,0:T(8,128)(2,1)S(1)}, bf16[256,2048]{1,0:T(8,128)(2,1)S(1)}, u32[]{:S(2)}, u32[]{:S(2)}) collective-permute-start(bf16[256,2048]{1,0:T(8,128)(2,1)S(1)} %copy-done.23), channel_id=1, source_target_pairs={{0,1},{3,2},{4,5},{7,6},{8,9},{11,10},{12,13},{15,14},{16,17},{19,... | collective-permute-start | bytes 3145736 | tf_op jit(solution)/shard_map/ppermute | solution.py:210
  537.3 60.1 %collective-permute-start.17 = (bf16[256,2048]{1,0:T(8,128)(2,1)S(1)}, bf16[256,2048]{1,0:T(8,128)(2,1)S(1)}, u32[]{:S(2)}, u32[]{:S(2)}) collective-permute-start(bf16[256,2048]{1,0:T(8,128)(2,1)S(1)} %copy-done.21), channel_id=1, source_target_pairs={{0,1},{3,2},{4,5},{7,6},{8,9},{11,10},{12,13},{15,14},{16,17},{19,... | collective-permute-start | bytes 3145736 | tf_op jit(solution)/shard_map/ppermute | solution.py:210
  544.3 54.3 %collective-permute-start.45 = (bf16[256,2048]{1,0:T(8,128)(2,1)S(1)}, bf16[256,2048]{1,0:T(8,128)(2,1)S(1)}, u32[]{:S(2)}, u32[]{:S(2)}) collective-permute-start(bf16[256,2048]{1,0:T(8,128)(2,1)S(1)} %add.252), channel_id=1, source_target_pairs={{1,0},{2,3},{5,4},{6,7},{9,8},{10,11},{13,12},{14,15},{17,16},{18,... | collective-permute-start | bytes 3145736 | tf_op jit(solution)/shard_map/ppermute | solution.py:210
  554.4 53.5 %collective-permute-start.44 = (bf16[256,2048]{1,0:T(8,128)(2,1)S(1)}, bf16[256,2048]{1,0:T(8,128)(2,1)S(1)}, u32[]{:S(2)}, u32[]{:S(2)}) collective-permute-start(bf16[256,2048]{1,0:T(8,128)(2,1)S(1)} %add.253), channel_id=1, source_target_pairs={{1,0},{2,3},{5,4},{6,7},{9,8},{10,11},{13,12},{14,15},{17,16},{18,... | collective-permute-start | bytes 3145736 | tf_op jit(solution)/shard_map/ppermute | solution.py:210
  556.5 71.8 %collective-permute-start.43 = (bf16[256,2048]{1,0:T(8,128)(2,1)S(1)}, bf16[256,2048]{1,0:T(8,128)(2,1)S(1)}, u32[]{:S(2)}, u32[]{:S(2)}) collective-permute-start(bf16[256,2048]{1,0:T(8,128)(2,1)S(1)} %add.254), channel_id=1, source_target_pairs={{1,0},{2,3},{5,4},{6,7},{9,8},{10,11},{13,12},{14,15},{17,16},{18,... | collective-permute-start | bytes 3145736 | tf_op jit(solution)/shard_map/ppermute | solution.py:210
  576.9 52.9 %collective-permute-start.28 = (bf16[256,2048]{1,0:T(8,128)(2,1)S(1)}, bf16[256,2048]{1,0:T(8,128)(2,1)S(1)}, u32[]{:S(2)}, u32[]{:S(2)}) collective-permute-start(bf16[256,2048]{1,0:T(8,128)(2,1)S(1)} %add.241), channel_id=1, source_target_pairs={{1,2},{2,1},{5,6},{6,5},{9,10},{10,9},{13,14},{14,13},{17,18},{18,... | collective-permute-start | bytes 3145736 | tf_op jit(solution)/shard_map/ppermute | solution.py:210
  631.7 48.7 %collective-permute-start.42 = (bf16[256,2048]{1,0:T(8,128)(2,1)S(1)}, bf16[256,2048]{1,0:T(8,128)(2,1)S(1)}, u32[]{:S(2)}, u32[]{:S(2)}) collective-permute-start(bf16[256,2048]{1,0:T(8,128)(2,1)S(1)} %add.255), channel_id=1, source_target_pairs={{1,0},{2,3},{5,4},{6,7},{9,8},{10,11},{13,12},{14,15},{17,16},{18,... | collective-permute-start | bytes 3145736 | tf_op jit(solution)/shard_map/ppermute | solution.py:210
  635.0 52.6 %collective-permute-start.41 = (bf16[256,2048]{1,0:T(8,128)(2,1)S(1)}, bf16[256,2048]{1,0:T(8,128)(2,1)S(1)}, u32[]{:S(2)}, u32[]{:S(2)}) collective-permute-start(bf16[256,2048]{1,0:T(8,128)(2,1)S(1)} %add.256), channel_id=1, source_target_pairs={{1,0},{2,3},{5,4},{6,7},{9,8},{10,11},{13,12},{14,15},{17,16},{18,... | collective-permute-start | bytes 3145736 | tf_op jit(solution)/shard_map/ppermute | solution.py:210
  636.7 66.3 %collective-permute-start.40 = (bf16[256,2048]{1,0:T(8,128)(2,1)S(1)}, bf16[256,2048]{1,0:T(8,128)(2,1)S(1)}, u32[]{:S(2)}, u32[]{:S(2)}) collective-permute-start(bf16[256,2048]{1,0:T(8,128)(2,1)S(1)} %add.257), channel_id=1, source_target_pairs={{1,0},{2,3},{5,4},{6,7},{9,8},{10,11},{13,12},{14,15},{17,16},{18,... | collective-permute-start | bytes 3145736 | tf_op jit(solution)/shard_map/ppermute | solution.py:210
  653.4 45.6 %collective-permute-start.25 = (bf16[256,2048]{1,0:T(8,128)(2,1)S(1)}, bf16[256,2048]{1,0:T(8,128)(2,1)S(1)}, u32[]{:S(2)}, u32[]{:S(2)}) collective-permute-start(bf16[256,2048]{1,0:T(8,128)(2,1)S(1)} %add.244), channel_id=1, source_target_pairs={{1,2},{2,1},{5,6},{6,5},{9,10},{10,9},{13,14},{14,13},{17,18},{18,... | collective-permute-start | bytes 3145736 | tf_op jit(solution)/shard_map/ppermute | solution.py:210
  687.6 52.3 %collective-permute-start.18 = (bf16[2048,384]{1,0:T(8,128)(2,1)}, bf16[2048,384]{1,0:T(8,128)(2,1)}, u32[]{:S(2)}, u32[]{:S(2)}) collective-permute-start(bf16[2048,384]{1,0:T(8,128)(2,1)} %convolution_convert_fusion.4), channel_id=1, source_target_pairs={{0,1},{3,2},{4,5},{7,6},{8,9},{11,10},{12,13},{15,14},{16,17},{19,... | collective-permute-start | bytes 4718600 | tf_op jit(solution)/shard_map/ppermute | solution.py:210
  704.4 46.7 %collective-permute-start.38 = (bf16[256,2048]{1,0:T(8,128)(2,1)}, bf16[256,2048]{1,0:T(8,128)(2,1)}, u32[]{:S(2)}, u32[]{:S(2)}) collective-permute-start(bf16[256,2048]{1,0:T(8,128)(2,1)} %add.259), channel_id=1, source_target_pairs={{1,0},{2,3},{5,4},{6,7},{9,8},{10,11},{13,12},{14,15},{17,16},{18,... | collective-permute-start | bytes 3145736 | tf_op jit(solution)/shard_map/ppermute | solution.py:210
  707.0 62.2 %collective-permute-start.37 = (bf16[256,2048]{1,0:T(8,128)(2,1)}, bf16[256,2048]{1,0:T(8,128)(2,1)}, u32[]{:S(2)}, u32[]{:S(2)}) collective-permute-start(bf16[256,2048]{1,0:T(8,128)(2,1)} %add.260), channel_id=1, source_target_pairs={{1,0},{2,3},{5,4},{6,7},{9,8},{10,11},{13,12},{14,15},{17,16},{18,... | collective-permute-start | bytes 3145736 | tf_op jit(solution)/shard_map/ppermute | solution.py:210
  775.5 60.7 %collective-permute-start.35 = (bf16[2048,384]{1,0:T(8,128)(2,1)}, bf16[2048,384]{1,0:T(8,128)(2,1)}, u32[]{:S(2)}, u32[]{:S(2)}) collective-permute-start(bf16[2048,384]{1,0:T(8,128)(2,1)} %add.262), channel_id=1, source_target_pairs={{1,0},{2,3},{5,4},{6,7},{9,8},{10,11},{13,12},{14,15},{17,16},{18,... | collective-permute-start | bytes 4718600 | tf_op jit(solution)/shard_map/ppermute | solution.py:210
  (100 other events, 1528.2 us)
Sparse Core Ops, SparseCore 0:
  9.9 57.0 all-gather.3
  68.9 40.9 all-gather.5
  111.8 73.2 all-gather.7
  289.1 70.3 reduce-scatter.6
  363.8 71.2 reduce-scatter.4
  483.4 55.6 reduce-scatter.10
  543.0 71.2 reduce-scatter.8
